TPU v7x, 32 devices: a whole 2x2x4 slice. The times are simulated.
32 devices in a mesh: rep: 8 (over z, core), rows: 4 (over y, x).
Axes of the slice: x: 2, y: 2, z: 4, core: 2. Of those that a mesh axis runs over, the one named last changes fastest.
Arguments:
- weights: bfloat16 [7168, 2048], P('rows'), may hold values from -6 to 6
- momentum: float32 [8, 7168, 2048], P('rep', 'rows'), may hold values from -8 to 8
- gradient: bfloat16 [8, 7168, 2048], P('rep', 'rows'), may hold values from -8 to 8
- right_factor: float32 [2048, 512], P('rows'), may hold values from -6 to 6
Outputs:
- new_weights: bfloat16 [7168, 2048], P('rows')
- new_momentum: float32 [8, 7168, 2048], P('rep', 'rows')
- new_right: float32 [2048, 512], P('rows')
All inputs are finite; a program needn't handle non-finite values.
Results may differ from a plain program's by a relative error of at most 0.019.
Values may be sent and summed in bfloat16 or wider, within the bound.
A program may use at most 128 MiB of HBM per device.

v0:
```python
import jax
import jax.numpy as jnp
from jax import lax
from jax.sharding import PartitionSpec as P

M = 7168
N = 2048
momentum_keep = 0.05
learn_rate = 0.5
tiny = 1e-06


def per_device(weights, momentum, gradient, right_factor):
    groups = lax.axis_size("rep")
    shards = lax.axis_size("rows")
    combined = momentum[0] + gradient[0].astype(jnp.float32)
    combined_half = combined.astype(jnp.bfloat16)
    columns = combined.shape[1]
    share = columns // shards
    left_local = jnp.dot(
        combined_half,
        lax.all_gather(right_factor.astype(jnp.bfloat16), "rows", axis=0, tiled=True),
        preferred_element_type=jnp.float32,
    )
    left_local = lax.optimization_barrier(left_local.astype(jnp.bfloat16)).astype(jnp.float32)
    left_mean = lax.psum(left_local.astype(jnp.bfloat16), "rep").astype(jnp.float32) / groups
    gram = lax.psum(jnp.dot(left_mean.T, left_mean, precision=lax.Precision.HIGHEST), "rows")
    chol = jnp.linalg.cholesky(gram)
    left_orth = jax.scipy.linalg.solve_triangular(chol, left_mean.T, lower=True).T
    left_half = left_orth.astype(jnp.bfloat16)
    partial_right = jnp.einsum(
        "ij,ik->jk", combined_half, left_half, preferred_element_type=jnp.float32
    )
    right_mean = lax.psum(partial_right, ("rep", "rows")) / groups
    normed = right_mean / jnp.sqrt(jnp.mean(right_mean * right_mean, axis=0) + tiny)
    feedback = jnp.dot(
        left_half, right_mean.astype(jnp.bfloat16).T, preferred_element_type=jnp.float32
    )
    update = jnp.dot(left_half, normed.astype(jnp.bfloat16).T, preferred_element_type=jnp.float32)
    new_right = lax.dynamic_slice_in_dim(normed, lax.axis_index("rows") * share, share, 0)
    new_momentum = combined - momentum_keep * feedback
    new_weights = (weights.astype(jnp.float32) - learn_rate * jnp.sqrt(M / N) * update).astype(
        jnp.bfloat16
    )
    return (new_weights, new_momentum[None], new_right)


def solution(mesh):
    in_specs = (P("rows", None), P("rep", "rows", None), P("rep", "rows", None), P("rows", None))
    out_specs = (P("rows", None), P("rep", "rows", None), P("rows", None))
    return jax.shard_map(
        per_device, mesh=mesh, in_specs=in_specs, out_specs=out_specs, check_vma=False
    )
```

profile of v0, /device:TPU:0, one launch (start us, length us, event | category | flops | bytes accessed | tf_op | source)
XLA Modules:
  0.0 525.9 jit_solution(10342217912073874617)
XLA Ops:
  7.2 0.0 all-gather.2.cloned.1.call-start
  7.2 2.1 convert_element_type.35
  9.3 0.0 all-reduce.5.cloned.1.call-start
  9.4 39.0 %all-gather.2.cloned.1.call-done = bf16[2048,512]{1,0:T(8,128)(2,1)} async-done(((bf16[512,512]{1,0:T(8,128)(2,1)}), bf16[2048,512]{1,0:T(8,128)(2,1)}) %all-gather.2.cloned.1.call-update) | async-done | bytes 2097168 | tf_op jit(solution)/shard_map/all_gather | solution.py:22
  48.3 13.1 %convolution_convert_fusion = bf16[1792,512]{1,0:T(8,128)(2,1)} fusion(bf16[2048,512]{1,0:T(8,128)(2,1)} %all-gather.2.cloned.1.call-done, f32[1,1792,2048]{2,1,0:T(8,128)} %param.5, bf16[1,1792,2048]{2,1,0:T(8,128)(2,1)} %param.6), kind=kOutput, calls=%fused_computation.13 | convolution fusion | flops 3770023936 | bytes 25952256 | tf_op jit(solution)/shard_map/dot_general | solution.py:20
  61.4 0.0 all-reduce.7.cloned.1.call-start
  61.5 63.3 %all-reduce.5.cloned.1.call-done = bf16[1792,512]{1,0:T(8,128)(2,1)} async-done(((bf16[1792,512]{1,0:T(8,128)(2,1)}), bf16[1792,512]{1,0:T(8,128)(2,1)}) %all-reduce.5.cloned.1.call-update) | async-done | bytes 1835024 | tf_op jit(solution)/shard_map/psum | solution.py:26
  124.7 9.4 %fusion.2 = f32[512,512]{0,1:T(8,128)} fusion(bf16[1792,512]{1,0:T(8,128)(2,1)} %all-reduce.5.cloned.1.call-done), kind=kOutput, calls=%fused_computation.12 | convolution fusion | flops 5638979584 | bytes 2883584 | tf_op jit(solution)/shard_map/dot_general | solution.py:27
  134.1 0.3 all-reduce.9.cloned.1.call-start
  134.4 2.4 fusion.1
  136.8 50.0 %all-reduce.7.cloned.1.call-done = f32[512,512]{0,1:T(8,128)} async-done(((f32[512,512]{0,1:T(8,128)}), f32[512,512]{0,1:T(8,128)}) %all-reduce.7.cloned.1.call-update) | async-done | bytes 1048592 | tf_op jit(solution)/shard_map/psum | solution.py:27
  186.8 1.6 copy.8
  188.3 1.4 fusion.18
  189.8 11.7 %cholesky.104 = f32[128,128]{1,0:T(8,128)S(1)} custom-call(f32[128,128]{1,0:T(8,128)S(1)} %cholesky.266), custom_call_target="Cholesky" | custom-call | tf_op jit(solution)/shard_map/jit(cholesky)/cholesky | solution.py:28
  201.5 9.8 %custom-call.31 = f32[1,128,128]{1,2,0:T(8,128)S(1)} custom-call(f32[1,128,128]{2,1,0:T(8,128)S(1)} %get-tuple-element.30), custom_call_target="InvertDiagBlocksLowerTriangular" | custom-call | tf_op jit(solution)/shard_map/jit(cholesky)/cholesky | solution.py:28
  211.4 0.1 cholesky.224
  211.5 0.3 constant_dynamic-update-slice_fusion.3
  211.8 0.3 convolution_subtract_fusion.2
  212.2 11.7 %cholesky.217 = f32[128,128]{1,0:T(8,128)S(1)} custom-call(f32[128,128]{1,0:T(8,128)S(1)} %cholesky.270), custom_call_target="Cholesky" | custom-call | tf_op jit(solution)/shard_map/jit(cholesky)/cholesky | solution.py:28
  223.9 10.2 %custom-call.32 = f32[1,128,128]{1,2,0:T(8,128)S(1)} custom-call(f32[1,128,128]{2,1,0:T(8,128)S(1)} %get-tuple-element.27), custom_call_target="InvertDiagBlocksLowerTriangular" | custom-call | tf_op jit(solution)/shard_map/jit(cholesky)/cholesky | solution.py:28
  234.2 0.3 convolution_dynamic-update-slice_fusion
  234.4 0.4 convolution_subtract_fusion.3
  234.8 11.7 %cholesky.238 = f32[128,128]{1,0:T(8,128)S(1)} custom-call(f32[128,128]{1,0:T(8,128)S(1)} %cholesky.275), custom_call_target="Cholesky" | custom-call | tf_op jit(solution)/shard_map/jit(cholesky)/cholesky | solution.py:28
  246.6 0.7 compare_reduce_fusion.1
  247.3 9.8 %custom-call.33 = f32[1,128,128]{1,2,0:T(8,128)S(1)} custom-call(f32[1,128,128]{2,1,0:T(8,128)S(1)} %get-tuple-element.24), custom_call_target="InvertDiagBlocksLowerTriangular" | custom-call | tf_op jit(solution)/shard_map/jit(cholesky)/cholesky | solution.py:28
  257.1 0.2 convolution_dynamic-update-slice_fusion.1
  257.3 0.4 convolution_subtract_fusion.4
  257.7 11.9 %cholesky.255 = f32[128,128]{1,0:T(8,128)S(1)} custom-call(f32[128,128]{1,0:T(8,128)S(1)} %convolution_subtract_fusion.4), custom_call_target="Cholesky" | custom-call | tf_op jit(solution)/shard_map/jit(cholesky)/cholesky | solution.py:28
  269.6 0.6 compare_reduce_fusion
  270.3 0.7 compare_reduce_fusion.2
  273.5 0.1 select_select_fusion
  273.6 8.5 %while.1 = (s32[]{:T(128)}, f32[512,512]{1,0:T(8,128)S(1)}, s32[4,2]{0,1:T(2,128)S(1)}, f32[4,128,128]{2,1,0:T(8,128)S(1)}, s32[]{:T(128)}) while((s32[]{:T(128)}, f32[512,512]{1,0:T(8,128)S(1)}, s32[4,2]{0,1:T(2,128)S(1)}, f32[4,128,128]{2,1,0:T(8,128)S(1)}, s32[]{:T(128)}) %tuple.34), condition=%wide.while_cond, body=%wide.while_body.sunk | while | flops 2 | bytes 131181 | solution.py:29
  273.6 0.1 constant_dynamic-slice_fusion.3
  273.7 0.6 fusion.53
  274.3 1.4 bitcast_dynamic-update-slice_fusion.2
  275.7 0.1 constant_dynamic-slice_fusion.3
  275.8 0.6 fusion.53
  276.4 1.4 bitcast_dynamic-update-slice_fusion.2
  277.9 0.1 constant_dynamic-slice_fusion.3
  277.9 0.6 fusion.53
  278.5 1.4 bitcast_dynamic-update-slice_fusion.2
  280.0 0.1 constant_dynamic-slice_fusion.3
  280.1 0.6 fusion.53
  280.6 1.4 bitcast_dynamic-update-slice_fusion.2
  282.1 39.3 %custom-call.34 = f32[4,128,128]{1,2,0:T(8,128)S(1)} custom-call(f32[4,128,128]{2,1,0:T(8,128)S(1)} %get-tuple-element.10), custom_call_target="InvertDiagBlocksLowerTriangular" | custom-call | tf_op jit(solution)/shard_map/jit(_solve_triangular)/triangular_solve | solution.py:29
  321.4 2.3 fusion.45
  323.7 2.8 convolution_subtract_fusion.1
  326.5 1.0 fusion.44
  327.5 3.2 convolution_subtract_fusion
  330.7 1.0 fusion.43
  331.7 4.7 fusion.9
  336.3 1.2 convolution_convert_fusion.1
  337.5 0.8 copy-done.5
  338.3 11.3 %fusion.41 = f32[2048,512]{1,0:T(8,128)} fusion(f32[1,1792,2048]{2,1,0:T(8,128)} %param.5, bf16[1,1792,2048]{2,1,0:T(8,128)(2,1)S(1)} %bitcast.67, bf16[128,1792]{1,0:T(8,128)(2,1)S(1)} %convolution_convert_fusion.1, bf16[128,1792]{1,0:T(8,128)(2,1)S(1)} %get-tuple-element.33, bf16[128,1792]{1,0:T(8,128)(2,1)S(1)} %get-tuple-element.35, ...), kind=kOutput, calls=%fused_computation.86 | convolution fusion | flops 3776446464 | bytes 28049408 | tf_op jit(solution)/shard_map/ij,ik->jk/dot_general | solution.py:31
  349.6 0.0 all-reduce.9.cloned.1.call-update
  349.6 142.5 %all-reduce.9.cloned.1.call-done = f32[2048,512]{1,0:T(8,128)} async-done(((f32[2048,512]{1,0:T(8,128)}), f32[2048,512]{1,0:T(8,128)}) %all-reduce.9.cloned.1.call-update) | async-done | bytes 4194320 | tf_op jit(solution)/shard_map/psum | solution.py:34
  492.1 2.9 multiply_reduce_fusion
  495.0 0.6 copy-done
  495.6 0.5 multiply_divide_fusion
  496.1 0.5 copy-done.4
  496.6 0.1 copy-done.6
  496.7 8.2 %subtract_convert_fusion = bf16[1792,2048]{1,0:T(8,128)(2,1)} fusion(bf16[1792,2048]{1,0:T(8,128)(2,1)} %param.4, f32[2048,512]{1,0:T(8,128)S(1)} %multiply_divide_fusion, bf16[128,1792]{1,0:T(8,128)(2,1)S(1)} %copy-done.6, bf16[128,1792]{1,0:T(8,128)(2,1)S(1)} %copy-done.4, bf16[128,1792]{1,0:T(8,128)(2,1)S(1)} %get-tuple-element.35, ...), kind=kOutput, calls=%fused_computation.5 | convolution fusion | flops 3781165056 | bytes 20709376 | tf_op jit(solution)/shard_map/dot_general | solution.py:39
  504.9 1.0 constant_dynamic-slice_fusion.1
  506.0 13.0 %fusion = f32[1,1792,2048]{2,1,0:T(8,128)} fusion(f32[1,1792,2048]{2,1,0:T(8,128)} %param.5, bf16[1,1792,2048]{2,1,0:T(8,128)(2,1)} %param.6, f32[2048,512]{1,0:T(8,128)S(1)} %copy-done, bf16[128,1792]{1,0:T(8,128)(2,1)} %copy-done.5, bf16[128,1792]{1,0:T(8,128)(2,1)} %copy-done.3, bf16[128,1792]{1,0:T(8,128)(2,1)S(1)} %get-tuple-element.35, ...), kind=kOutput, calls=%fused_computation.4 | convolution fusion | flops 3782213632 | bytes 42729472 | tf_op jit(solution)/shard_map/dot_general | solution.py:36
  (29 shorter events, 0.3 us)
Async XLA Ops:
  7.2 41.2 %all-gather.2.cloned.1.call-start = ((), (), s32[]{:S(2)}) async-start(), calls=%async_computation | async-start | bytes 2621440 | tf_op jit(solution)/shard_map/all_gather | solution.py:22
  9.3 115.4 %all-reduce.5.cloned.1.call-start = ((), (), s32[]{:S(2)}) async-start(), calls=%async_computation.1 | async-start | bytes 3670016 | tf_op jit(solution)/shard_map/psum | solution.py:26
  61.4 125.4 %all-reduce.7.cloned.1.call-start = ((), (), s32[]{:S(2)}) async-start(), calls=%async_computation.2 | async-start | bytes 2097152 | tf_op jit(solution)/shard_map/psum | solution.py:27
  124.7 9.7 %copy-start.2 = (bf16[1792,512]{1,0:T(8,128)(2,1)S(1)}, bf16[1792,512]{1,0:T(8,128)(2,1)}, u32[]{:S(2)}) copy-start(bf16[1792,512]{1,0:T(8,128)(2,1)} %all-reduce.5.cloned.1.call-done) | copy-start | bytes 5505028
  134.1 358.0 %all-reduce.9.cloned.1.call-start = ((), (), s32[]{:S(2)}) async-start(), calls=%async_computation.3 | async-start | bytes 8388608 | tf_op jit(solution)/shard_map/psum | solution.py:34
  321.4 6.1 %copy-start.1 = (f32[512,1792]{0,1:T(8,128)S(1)}, f32[512,1792]{0,1:T(8,128)}, u32[]{:S(2)}) copy-start(f32[512,1792]{0,1:T(8,128)} %fusion.1) | copy-start | bytes 11010052
  326.5 11.8 %slice-start = ((s8[7340032]{0:T(1024)(128)(4,1)}), s8[4194304]{0:T(1024)(128)(4,1)S(1)}, s32[]{:S(2)}) async-start(s8[7340032]{0:T(1024)(128)(4,1)} %bitcast.66), calls=%async_computation.4 | async-start | bytes 8388608
  330.7 7.6 %slice-start.1 = ((s8[7340032]{0:T(1024)(128)(4,1)}), s8[3145728]{0:T(1024)(128)(4,1)S(1)}, s32[]{:S(2)}) async-start(s8[7340032]{0:T(1024)(128)(4,1)} %bitcast.66), calls=%async_computation.5 | async-start | bytes 6291456
  331.7 17.9 %copy-start.3 = (bf16[128,1792]{1,0:T(8,128)(2,1)}, bf16[128,1792]{1,0:T(8,128)(2,1)S(1)}, u32[]{:S(2)}) copy-start(bf16[128,1792]{1,0:T(8,128)(2,1)S(1)} %get-tuple-element.33) | copy-start | bytes 1376260
  337.5 0.8 copy-start.5
  492.1 3.4 copy-start
  495.6 1.0 copy-start.4
  495.6 1.2 copy-start.6
Sparse Core Ops, SparseCore 0:
  10.4 37.8 all-gather.1
  61.5 63.1 all-reduce.4
  134.3 52.4 all-reduce.6
  349.7 142.3 all-reduce.8
where the time goes:
time: 534 us; the launch traced here: 526 us
  waiting for transfers between devices  295 us (55%)
  other arithmetic  128 us (24%)
  matrix products  72.8 us (14%)
  between operations  17 us (3%)
  local copies, waits for them, and re-layouts  13.1 us (2%)
    psum x1, waiting for transfers between devices, per_device(): right_mean = lax.psum(partial_right, ('rep', 'rows')) / groups  143 us
    another operation x14, other arithmetic, per_device(): chol = jnp.linalg.cholesky(gram)  79 us
    psum x1, waiting for transfers between devices, per_device(): lax.psum(left_local.astype(jnp.bfloat16), 'rep').astype(jnp.float32)  63.3 us
    psum x1, waiting for transfers between devices, per_device(): lax.psum(jnp.dot(left_mean.T, left_mean, precision=lax.Precision.HIGHEST)...  50 us
    another operation x3, other arithmetic, per_device(): jax.scipy.linalg.solve_triangular(chol, left_mean.T, lower=True)  39.4 us
    all_gather x1, waiting for transfers between devices, per_device(): lax.all_gather(right_factor.astype(jnp.bfloat16), 'rows', axis=0, tiled=T...  39 us
    another operation x7, matrix products, per_device(): jax.scipy.linalg.solve_triangular(chol, left_mean.T, lower=True)  16 us
    dot_general x1, matrix products, per_device(): jnp.dot(combined_half, lax.all_gather(right_factor.astype(jnp.bfloat16),...  13.1 us
  transfers between devices with their start and end apart: 4, of which 4 were waited for; matrix products, arithmetic and copies ran while one was open for 0% of the time, Pallas kernels for 0%

commit v1 on v0

--- a/solution.py
+++ b/solution.py
@@ -23,7 +23,8 @@
         preferred_element_type=jnp.float32,
     )
     left_local = lax.optimization_barrier(left_local.astype(jnp.bfloat16)).astype(jnp.float32)
-    left_mean = lax.psum(left_local.astype(jnp.bfloat16), "rep").astype(jnp.float32) / groups
+    _track_map = lambda incoming_x, ax_name: jnp.sum(lax.all_gather(incoming_x, ax_name), axis=0)
+    left_mean = _track_map(left_local.astype(jnp.bfloat16), "rep").astype(jnp.float32) / groups
     gram = lax.psum(jnp.dot(left_mean.T, left_mean, precision=lax.Precision.HIGHEST), "rows")
     chol = jnp.linalg.cholesky(gram)
     left_orth = jax.scipy.linalg.solve_triangular(chol, left_mean.T, lower=True).T

time: 534 us -> 605 us (1.13)
  waiting for transfers between devices: 295 us -> 363 us
  other arithmetic: 128 us -> 136 us
    all_gather x0 -> x1, waiting for transfers between devices: none -> 134 us  [per_device(): lax.all_gather(incoming_x, ax_name)]
    psum x1 -> x0, waiting for transfers between devices: 63.3 us -> none  [per_device(): lax.psum(left_local.astype(jnp.bfloat16), 'rep').astype(jnp.float32)]
    reduce_sum x0 -> x1, other arithmetic: none -> 8.52 us  [per_device(): jnp.sum(lax.all_gather(incoming_x, ax_name), axis=0)]
where the time goes in v1:
time: 605 us; the launch traced here: 601 us
  waiting for transfers between devices  363 us (60%)
  other arithmetic  136 us (22%)
  matrix products  70.6 us (12%)
  between operations  16.8 us (3%)
  local copies, waits for them, and re-layouts  13.1 us (2%)
    psum x1, waiting for transfers between devices, per_device(): right_mean = lax.psum(partial_right, ('rep', 'rows')) / groups  143 us
    all_gather x1, waiting for transfers between devices, per_device(): lax.all_gather(incoming_x, ax_name)  134 us
    another operation x14, other arithmetic, per_device(): chol = jnp.linalg.cholesky(gram)  79 us
    psum x1, waiting for transfers between devices, per_device(): lax.psum(jnp.dot(left_mean.T, left_mean, precision=lax.Precision.HIGHEST)...  48.2 us
    another operation x3, other arithmetic, per_device(): jax.scipy.linalg.solve_triangular(chol, left_mean.T, lower=True)  39.4 us
    all_gather x1, waiting for transfers between devices, per_device(): lax.all_gather(right_factor.astype(jnp.bfloat16), 'rows', axis=0, tiled=T...  39 us
    another operation x7, matrix products, per_device(): jax.scipy.linalg.solve_triangular(chol, left_mean.T, lower=True)  16 us
    dot_general x1, matrix products, per_device(): jnp.dot(combined_half, lax.all_gather(right_factor.astype(jnp.bfloat16),...  13.1 us
  transfers between devices with their start and end apart: 4, of which 4 were waited for; matrix products, arithmetic and copies ran while one was open for 0% of the time, Pallas kernels for 0%

profile of v1, /device:TPU:0, one launch (start us, length us, event | category | flops | bytes accessed | tf_op | source)
XLA Modules:
  0.0 601.0 jit_solution(4330169185956516917)
XLA Ops:
  7.2 0.0 all-gather.4.cloned.1.call-start
  7.2 2.1 convert_element_type.39
  9.3 0.0 all-gather.6.cloned.1.call-start
  9.4 39.0 %all-gather.4.cloned.1.call-done = bf16[2048,512]{1,0:T(8,128)(2,1)} async-done(((bf16[512,512]{1,0:T(8,128)(2,1)}), bf16[2048,512]{1,0:T(8,128)(2,1)}) %all-gather.4.cloned.1.call-update) | async-done | bytes 2097168 | tf_op jit(solution)/shard_map/all_gather | solution.py:22
  48.3 13.1 %convolution_convert_fusion = bf16[1792,512]{1,0:T(8,128)(2,1)} fusion(bf16[2048,512]{1,0:T(8,128)(2,1)} %all-gather.4.cloned.1.call-done, f32[1,1792,2048]{2,1,0:T(8,128)} %param.5, bf16[1,1792,2048]{2,1,0:T(8,128)(2,1)} %param.6), kind=kOutput, calls=%fused_computation.13 | convolution fusion | flops 3770023936 | bytes 25952256 | tf_op jit(solution)/shard_map/dot_general | solution.py:20
  61.4 0.5 all-reduce.4.cloned.1.call-start
  61.9 133.5 %all-gather.6.cloned.1.call-done = bf16[14336,512]{1,0:T(8,128)(2,1)} async-done(((bf16[1792,512]{1,0:T(8,128)(2,1)}), bf16[14336,512]{1,0:T(8,128)(2,1)}) %all-gather.6.cloned.1.call-update) | async-done | bytes 14680080 | tf_op jit(solution)/shard_map/all_gather | solution.py:26
  195.5 8.5 %reduce_sum.21 = bf16[1792,512]{1,0:T(8,128)(2,1)S(1)} reduce(bf16[8,1792,512]{2,1,0:T(8,128)(2,1)} %bitcast.67, bf16[]{:T(256)} %constant.155.clone.1), dimensions={0}, to_apply=%region_0.0 | reduce | flops 6422528 | bytes 16515074 | tf_op jit(solution)/shard_map/reduce_sum | solution.py:26
  204.0 7.2 %fusion.2 = f32[512,512]{0,1:T(8,128)} fusion(bf16[1792,512]{1,0:T(8,128)(2,1)S(1)} %reduce_sum.21), kind=kOutput, calls=%fused_computation.12 | convolution fusion | flops 5638979584 | bytes 2883584 | tf_op jit(solution)/shard_map/dot_general | solution.py:28
  211.2 0.2 all-reduce.6.cloned.1.call-start
  211.4 2.4 fusion.1
  213.8 48.2 %all-reduce.4.cloned.1.call-done = f32[512,512]{0,1:T(8,128)} async-done(((f32[512,512]{0,1:T(8,128)}), f32[512,512]{0,1:T(8,128)}) %all-reduce.4.cloned.1.call-update) | async-done | bytes 1048592 | tf_op jit(solution)/shard_map/psum | solution.py:28
  262.0 1.6 copy.8
  263.5 1.4 fusion.18
  265.0 11.7 %cholesky.104 = f32[128,128]{1,0:T(8,128)S(1)} custom-call(f32[128,128]{1,0:T(8,128)S(1)} %cholesky.266), custom_call_target="Cholesky" | custom-call | tf_op jit(solution)/shard_map/jit(cholesky)/cholesky | solution.py:29
  276.7 9.8 %custom-call.31 = f32[1,128,128]{1,2,0:T(8,128)S(1)} custom-call(f32[1,128,128]{2,1,0:T(8,128)S(1)} %get-tuple-element.30), custom_call_target="InvertDiagBlocksLowerTriangular" | custom-call | tf_op jit(solution)/shard_map/jit(cholesky)/cholesky | solution.py:29
  286.6 0.1 cholesky.224
  286.7 0.3 constant_dynamic-update-slice_fusion.3
  287.0 0.3 convolution_subtract_fusion.2
  287.3 11.7 %cholesky.217 = f32[128,128]{1,0:T(8,128)S(1)} custom-call(f32[128,128]{1,0:T(8,128)S(1)} %cholesky.270), custom_call_target="Cholesky" | custom-call | tf_op jit(solution)/shard_map/jit(cholesky)/cholesky | solution.py:29
  299.1 10.2 %custom-call.32 = f32[1,128,128]{1,2,0:T(8,128)S(1)} custom-call(f32[1,128,128]{2,1,0:T(8,128)S(1)} %get-tuple-element.27), custom_call_target="InvertDiagBlocksLowerTriangular" | custom-call | tf_op jit(solution)/shard_map/jit(cholesky)/cholesky | solution.py:29
  309.3 0.3 convolution_dynamic-update-slice_fusion
  309.6 0.4 convolution_subtract_fusion.3
  310.0 11.7 %cholesky.238 = f32[128,128]{1,0:T(8,128)S(1)} custom-call(f32[128,128]{1,0:T(8,128)S(1)} %cholesky.275), custom_call_target="Cholesky" | custom-call | tf_op jit(solution)/shard_map/jit(cholesky)/cholesky | solution.py:29
  321.7 0.7 compare_reduce_fusion.1
  322.4 9.8 %custom-call.33 = f32[1,128,128]{1,2,0:T(8,128)S(1)} custom-call(f32[1,128,128]{2,1,0:T(8,128)S(1)} %get-tuple-element.24), custom_call_target="InvertDiagBlocksLowerTriangular" | custom-call | tf_op jit(solution)/shard_map/jit(cholesky)/cholesky | solution.py:29
  332.2 0.2 convolution_dynamic-update-slice_fusion.1
  332.5 0.4 convolution_subtract_fusion.4
  332.8 11.9 %cholesky.255 = f32[128,128]{1,0:T(8,128)S(1)} custom-call(f32[128,128]{1,0:T(8,128)S(1)} %convolution_subtract_fusion.4), custom_call_target="Cholesky" | custom-call | tf_op jit(solution)/shard_map/jit(cholesky)/cholesky | solution.py:29
  344.8 0.6 compare_reduce_fusion
  345.4 0.7 compare_reduce_fusion.2
  348.6 0.1 select_select_fusion
  348.7 8.5 %while.1 = (s32[]{:T(128)}, f32[512,512]{1,0:T(8,128)S(1)}, s32[4,2]{0,1:T(2,128)S(1)}, f32[4,128,128]{2,1,0:T(8,128)S(1)}, s32[]{:T(128)}) while((s32[]{:T(128)}, f32[512,512]{1,0:T(8,128)S(1)}, s32[4,2]{0,1:T(2,128)S(1)}, f32[4,128,128]{2,1,0:T(8,128)S(1)}, s32[]{:T(128)}) %tuple.34), condition=%wide.while_cond, body=%wide.while_body.sunk | while | flops 2 | bytes 131181 | solution.py:30
  348.8 0.1 constant_dynamic-slice_fusion.3
  348.8 0.6 fusion.53
  349.4 1.4 bitcast_dynamic-update-slice_fusion.2
  350.9 0.1 constant_dynamic-slice_fusion.3
  351.0 0.6 fusion.53
  351.5 1.4 bitcast_dynamic-update-slice_fusion.2
  353.0 0.1 constant_dynamic-slice_fusion.3
  353.1 0.6 fusion.53
  353.7 1.4 bitcast_dynamic-update-slice_fusion.2
  355.1 0.1 constant_dynamic-slice_fusion.3
  355.2 0.6 fusion.53
  355.8 1.4 bitcast_dynamic-update-slice_fusion.2
  357.2 39.3 %custom-call.34 = f32[4,128,128]{1,2,0:T(8,128)S(1)} custom-call(f32[4,128,128]{2,1,0:T(8,128)S(1)} %get-tuple-element.10), custom_call_target="InvertDiagBlocksLowerTriangular" | custom-call | tf_op jit(solution)/shard_map/jit(_solve_triangular)/triangular_solve | solution.py:30
  396.6 2.3 fusion.45
  398.9 2.8 convolution_subtract_fusion.1
  401.7 1.0 fusion.44
  402.6 3.2 convolution_subtract_fusion
  405.8 1.0 fusion.43
  406.8 4.7 fusion.9
  411.5 1.2 convolution_convert_fusion.1
  412.7 0.8 copy-done.4
  413.4 11.3 %fusion.41 = f32[2048,512]{1,0:T(8,128)} fusion(f32[1,1792,2048]{2,1,0:T(8,128)} %param.5, bf16[1,1792,2048]{2,1,0:T(8,128)(2,1)S(1)} %bitcast.69, bf16[128,1792]{1,0:T(8,128)(2,1)S(1)} %convolution_convert_fusion.1, bf16[128,1792]{1,0:T(8,128)(2,1)S(1)} %get-tuple-element.33, bf16[128,1792]{1,0:T(8,128)(2,1)S(1)} %get-tuple-element.35, ...), kind=kOutput, calls=%fused_computation.86 | convolution fusion | flops 3776446464 | bytes 28049408 | tf_op jit(solution)/shard_map/ij,ik->jk/dot_general | solution.py:32
  424.7 142.7 %all-reduce.6.cloned.1.call-done = f32[2048,512]{1,0:T(8,128)} async-done(((f32[2048,512]{1,0:T(8,128)}), f32[2048,512]{1,0:T(8,128)}) %all-reduce.6.cloned.1.call-update) | async-done | bytes 4194320 | tf_op jit(solution)/shard_map/psum | solution.py:35
  567.4 2.9 multiply_reduce_fusion
  570.3 0.6 copy-done
  570.9 0.5 multiply_divide_fusion
  571.4 0.5 copy-done.3
  571.9 0.1 copy-done.5
  572.0 8.2 %subtract_convert_fusion = bf16[1792,2048]{1,0:T(8,128)(2,1)} fusion(bf16[1792,2048]{1,0:T(8,128)(2,1)} %param.4, f32[2048,512]{1,0:T(8,128)S(1)} %multiply_divide_fusion, bf16[128,1792]{1,0:T(8,128)(2,1)S(1)} %copy-done.5, bf16[128,1792]{1,0:T(8,128)(2,1)S(1)} %copy-done.3, bf16[128,1792]{1,0:T(8,128)(2,1)S(1)} %get-tuple-element.35, ...), kind=kOutput, calls=%fused_computation.5 | convolution fusion | flops 3781165056 | bytes 20709376 | tf_op jit(solution)/shard_map/dot_general | solution.py:40
  580.2 1.0 constant_dynamic-slice_fusion.1
  581.3 13.0 %fusion = f32[1,1792,2048]{2,1,0:T(8,128)} fusion(f32[1,1792,2048]{2,1,0:T(8,128)} %param.5, bf16[1,1792,2048]{2,1,0:T(8,128)(2,1)} %param.6, f32[2048,512]{1,0:T(8,128)S(1)} %copy-done, bf16[128,1792]{1,0:T(8,128)(2,1)} %copy-done.4, bf16[128,1792]{1,0:T(8,128)(2,1)} %copy-done.2, bf16[128,1792]{1,0:T(8,128)(2,1)S(1)} %get-tuple-element.35, ...), kind=kOutput, calls=%fused_computation.4 | convolution fusion | flops 3782213632 | bytes 42729472 | tf_op jit(solution)/shard_map/dot_general | solution.py:37
  (28 shorter events, 0.3 us)
Async XLA Ops:
  7.2 41.2 %all-gather.4.cloned.1.call-start = ((), (), s32[]{:S(2)}) async-start(), calls=%async_computation | async-start | bytes 2621440 | tf_op jit(solution)/shard_map/all_gather | solution.py:22
  9.3 186.1 %all-gather.6.cloned.1.call-start = ((), (), s32[]{:S(2)}) async-start(), calls=%async_computation.3 | async-start | bytes 16515072 | tf_op jit(solution)/shard_map/all_gather | solution.py:26
  61.4 200.5 %all-reduce.4.cloned.1.call-start = ((), (), s32[]{:S(2)}) async-start(), calls=%async_computation.1 | async-start | bytes 2097152 | tf_op jit(solution)/shard_map/psum | solution.py:28
  211.2 356.3 %all-reduce.6.cloned.1.call-start = ((), (), s32[]{:S(2)}) async-start(), calls=%async_computation.2 | async-start | bytes 8388608 | tf_op jit(solution)/shard_map/psum | solution.py:35
  396.6 6.1 %copy-start.1 = (f32[512,1792]{0,1:T(8,128)S(1)}, f32[512,1792]{0,1:T(8,128)}, u32[]{:S(2)}) copy-start(f32[512,1792]{0,1:T(8,128)} %fusion.1) | copy-start | bytes 11010052
  401.7 11.8 %slice-start = ((s8[7340032]{0:T(1024)(128)(4,1)}), s8[4194304]{0:T(1024)(128)(4,1)S(1)}, s32[]{:S(2)}) async-start(s8[7340032]{0:T(1024)(128)(4,1)} %bitcast.68), calls=%async_computation.4 | async-start | bytes 8388608
  405.8 7.6 %slice-start.1 = ((s8[7340032]{0:T(1024)(128)(4,1)}), s8[3145728]{0:T(1024)(128)(4,1)S(1)}, s32[]{:S(2)}) async-start(s8[7340032]{0:T(1024)(128)(4,1)} %bitcast.68), calls=%async_computation.5 | async-start | bytes 6291456
  406.8 17.9 %copy-start.2 = (bf16[128,1792]{1,0:T(8,128)(2,1)}, bf16[128,1792]{1,0:T(8,128)(2,1)S(1)}, u32[]{:S(2)}) copy-start(bf16[128,1792]{1,0:T(8,128)(2,1)S(1)} %get-tuple-element.33) | copy-start | bytes 1376260
  412.7 0.8 copy-start.4
  567.4 3.4 copy-start
  570.9 1.0 copy-start.3
  570.9 1.2 copy-start.5
Sparse Core Ops, SparseCore 0:
  10.4 37.8 all-gather.3
  61.5 133.8 all-gather.5
  211.3 50.6 all-reduce.3
  424.9 142.5 all-reduce.5
